TPU v7x, 32 devices: a whole 2x2x4 slice. The times are simulated.
32 devices in a mesh: grp: 2 (over x), had: 16 (over z, y, core).
Axes of the slice: x: 2, y: 2, z: 4, core: 2. Of those that a mesh axis runs over, the one named last changes fastest.
Arguments:
- source_slabs: bfloat16 [512, 128, 128], P(('grp', 'had')), parts along dimension 0, may hold values from -6 to 6
- sink_slabs: bfloat16 [512, 128, 128], P(('grp', 'had')), parts along dimension 0, may hold values from -6 to 6
- perambulators: bfloat16 [4, 2, 128, 128], P('grp'), parts along dimension 0, may hold values from -0.5 to 0.5
- send_pick: int32 [32, 16], P(('grp', 'had')), parts along dimension 0, may hold values from 0 to 15
- graph_slot: int32 [32, 512, 2], P(('grp', 'had')), parts along dimension 0, may hold values from 0 to 15
- graph_sink: int32 [32, 512, 2], P(('grp', 'had')), parts along dimension 0, may hold values from 0 to 15
- graph_count: int32 [32], P(('grp', 'had')), parts along dimension 0, may hold values from 64 to 512, as said below
- pair_list: int32 [256, 2], P(('grp', 'had')), parts along dimension 0, may hold values from 0 to 15
Outputs:
- edge_matrices: bfloat16 [32, 128, 128], P(('grp', 'had')), parts along dimension 0
- pair_products: bfloat16 [256, 128, 128], P(('grp', 'had')), parts along dimension 0
There are 2 independent parts, one for each index of `grp`. A program takes and returns all parts, laid end to end along the dimension named above; each array names one. Nothing has to cross between parts.
Inputs may be any that keep to these rules, and one draw needn't show every extreme that they name: Some reader uses all 512 graph slots; slots from graph_count on are unused.
All inputs are finite; a program needn't handle non-finite values.
Results may differ from a plain program's by a relative error of at most 0.012.
Values may be sent and summed in bfloat16 or wider, within the bound.
A program may use at most 64 MiB of HBM per device.

v0:
```python
import math

import jax
import jax.numpy as jnp
from jax import lax
from jax.sharding import PartitionSpec as P


def shards(
    source_slabs,
    sink_slabs,
    perambulators,
    send_pick,
    graph_slot,
    graph_sink,
    graph_count,
    pair_list,
):
    my_index = lax.axis_index("had")
    evecs = source_slabs.shape[1]
    per_device = source_slabs.shape[0]
    root_scale = 1.0 / math.sqrt(evecs)
    edge_scale = 1.0 / math.sqrt(evecs * graph_slot.shape[1])
    timeslice = my_index * per_device // evecs
    local_peram = lax.dynamic_index_in_dim(perambulators, timeslice, 0, keepdims=False)
    first_turn = jnp.einsum(
        "xa,jab->xjb", local_peram[0], source_slabs, preferred_element_type=jnp.float32
    ).astype(jnp.bfloat16)
    pick_row = send_pick[0]
    second_turn = jnp.einsum(
        "xjb,yb->xjy", first_turn, local_peram[1], preferred_element_type=jnp.float32
    ).astype(jnp.bfloat16)
    outgoing = jnp.take(second_turn, pick_row, axis=1)
    received = lax.all_to_all(outgoing, "had", split_axis=1, concat_axis=1, tiled=True)
    graph_rows = graph_slot.shape[1]
    block_width = min(64, graph_rows)
    slot_table = graph_slot[0]
    sink_table = graph_sink[0]
    graph_total = graph_count[0]

    def factor(slots, sinks):
        gathered = jnp.take(received, slots, axis=1)
        resident = jnp.take(sink_slabs, sinks, axis=0)
        product = jnp.einsum("gxb,agb->gxa", resident, gathered, preferred_element_type=jnp.float32)
        return (product * root_scale).astype(jnp.bfloat16)

    def accumulate(block_index, running_sum):
        offset = block_index * block_width
        slots = lax.dynamic_slice_in_dim(slot_table, offset, block_width, 0)
        sinks = lax.dynamic_slice_in_dim(sink_table, offset, block_width, 0)
        is_valid = (offset + jnp.arange(block_width, dtype=jnp.int32) < graph_total).astype(
            jnp.bfloat16
        )
        left_side = factor(slots[:, 0], sinks[:, 0]) * is_valid[:, None, None]
        right_side = factor(slots[:, 1], sinks[:, 1])
        return running_sum + jnp.einsum(
            "gxa,gay->xy", left_side, right_side, preferred_element_type=jnp.float32
        )

    block_count = (graph_total + block_width - 1) // block_width
    summed = lax.fori_loop(0, block_count, accumulate, jnp.zeros((evecs, evecs), jnp.float32))
    edge_local = (summed * edge_scale).astype(jnp.bfloat16)[None]
    left_ids = pair_list[:, 0]
    right_ids = pair_list[:, 1]
    shard_rows = lax.all_gather(edge_local, "had", axis=0, tiled=True)
    row_ids = jnp.arange(shard_rows.shape[0], dtype=jnp.int32)
    left_select = (left_ids[:, None] == row_ids[None, :]).astype(jnp.bfloat16)
    right_select = (right_ids[:, None] == row_ids[None, :]).astype(jnp.bfloat16)
    left_part = jnp.einsum(
        "pn,nxy->pxy", left_select, shard_rows, preferred_element_type=jnp.float32
    )
    right_part = jnp.einsum(
        "pn,nxy->pxy", right_select, shard_rows, preferred_element_type=jnp.float32
    )
    left_edges = left_part.astype(jnp.bfloat16)
    right_edges = right_part.astype(jnp.bfloat16)
    product = jnp.einsum(
        "pxa,pay->pxy", left_edges, right_edges, preferred_element_type=jnp.float32
    )
    pair_products = (product * root_scale).astype(jnp.bfloat16)
    return (edge_local, pair_products)


def solution(mesh):
    return jax.shard_map(
        shards,
        mesh=mesh,
        in_specs=(
            P(("grp", "had"), None, None),
            P(("grp", "had"), None, None),
            P("grp", None, None, None),
            P(("grp", "had"), None),
            P(("grp", "had"), None, None),
            P(("grp", "had"), None, None),
            P(("grp", "had")),
            P(("grp", "had"), None),
        ),
        out_specs=(P(("grp", "had"), None, None), P(("grp", "had"), None, None)),
        check_vma=False,
    )
```

profile of v0, /device:TPU:0, one launch (start us, length us, event | category | flops | bytes accessed | tf_op | source)
XLA Modules:
  0.0 211.1 jit_solution(10187311681063074676)
XLA Ops:
  5.0 7.4 %all-to-all-start = ((bf16[128,16,128]{2,0,1:T(8,128)(2,1)}), bf16[128,16,128]{2,0,1:T(8,128)(2,1)S(1)}, u32[]{:S(2)}, u32[]{:S(2)}) async-start(bf16[128,16,128]{2,0,1:T(8,128)(2,1)} %select_bitcast_fusion), calls=%async_computation | async-start | bytes 1048576 | tf_op jit(solution)/shard_map/all_to_all | solution.py:34
  13.1 13.6 %all-to-all-done = bf16[128,16,128]{2,0,1:T(8,128)(2,1)S(1)} async-done(((bf16[128,16,128]{2,0,1:T(8,128)(2,1)}), bf16[128,16,128]{2,0,1:T(8,128)(2,1)S(1)}, u32[]{:S(2)}, u32[]{:S(2)}) %all-to-all-start) | async-done | bytes 524320 | tf_op jit(solution)/shard_map/all_to_all | solution.py:34
  26.7 81.4 %while.10 = (s32[]{:T(128)}, f32[128,128]{1,0:T(8,128)S(1)}, s32[]{:T(128)}, s32[512,2]{0,1:T(2,128)}, bf16[16,128,128]{2,1,0:T(8,128)(2,1)S(1)}, /*index=5*/s32...) while((s32[]{:T(128)}, f32[128,128]{1,0:T(8,128)S(1)}, ...), condition=%wide.region_1.4_spmd, body=%wide.region_0.3_spmd.sunk | while | flops 814765760 | bytes 29514672 | solution.py:61
  27.5 2.1 %gather_fusion = bf16[64,128,128]{2,1,0:T(8,128)(2,1)} fusion(bf16[128,16,128]{2,0,1:T(8,128)(2,1)S(1)} %get-tuple-element.188, s32[1024]{0:T(1024)S(1)} %pad_clamp_fusion.9), kind=kCustom, calls=%fused_computation.3.clone.clone.1 | custom fusion | bytes 4194560 | tf_op jit(solution)/shard_map/while/body/jit(_take)/gather | solution.py:42
  29.7 2.1 %gather_fusion.1 = bf16[64,128,128]{2,1,0:T(8,128)(2,1)} fusion(bf16[16,128,128]{2,1,0:T(8,128)(2,1)S(1)} %get-tuple-element.186, s32[1024]{0:T(1024)S(1)} %pad_clamp_fusion.10), kind=kCustom, calls=%fused_computation.2.clone.clone.1 | custom fusion | bytes 4194560 | tf_op jit(solution)/shard_map/while/body/jit(_take)/gather | solution.py:43
  31.8 5.2 %multiply_convert_fusion.4 = bf16[64,128,128]{2,1,0:T(8,128)(2,1)} fusion(bf16[64,128,128]{2,1,0:T(8,128)(2,1)} %gather_fusion, bf16[64,128,128]{2,1,0:T(8,128)(2,1)} %gather_fusion.1, pred[64]{0:T(512)(128)(4,1)S(1)} %get-tuple-element.152, pred[64]{0:T(512)(128)(4,1)S(1)} %get-tuple-element.153), kind=kOutput, calls=%fused_computation.5.clone.1 | convolution fusion | flops 272629760 | bytes 6291584 | tf_op jit(solution)/shard_map/while/body/gxb,agb->gxa/dot_general | solution.py:44
  39.1 2.1 %gather_fusion.3 = bf16[64,128,128]{2,1,0:T(8,128)(2,1)} fusion(bf16[16,128,128]{2,1,0:T(8,128)(2,1)S(1)} %get-tuple-element.186, s32[1024]{0:T(1024)S(1)} %pad_clamp_fusion.12), kind=kCustom, calls=%fused_computation.clone.clone.1 | custom fusion | bytes 4194560 | tf_op jit(solution)/shard_map/while/body/jit(_take)/gather | solution.py:43
  41.9 5.1 %fusion.64 = f32[128,128]{1,0:T(8,128)S(1)} fusion(f32[128,128]{1,0:T(8,128)S(1)} %get-tuple-element.171, bf16[64,128,128]{2,1,0:T(8,128)(2,1)} %multiply_convert_fusion.4, bf16[64,128,128]{2,1,0:T(8,128)(2,1)} %gather_fusion.2, bf16[64,128,128]{2,1,0:T(8,128)(2,1)} %gather_fusion.3, pred[64]{0:T(512)(128)(4,1)S(1)} %get-tuple-element.156, ...), kind=kOutput, calls=%fused_computation.20.clone.1 | convolution fusion | flops 542130176 | bytes 6422784 | tf_op jit(solution)/shard_map/while/body/gxa,gay->xy/dot_general | solution.py:56
  47.9 2.1 %gather_fusion = bf16[64,128,128]{2,1,0:T(8,128)(2,1)} fusion(bf16[128,16,128]{2,0,1:T(8,128)(2,1)S(1)} %get-tuple-element.188, s32[1024]{0:T(1024)S(1)} %pad_clamp_fusion.9), kind=kCustom, calls=%fused_computation.3.clone.clone.1 | custom fusion | bytes 4194560 | tf_op jit(solution)/shard_map/while/body/jit(_take)/gather | solution.py:42
  50.0 2.1 %gather_fusion.1 = bf16[64,128,128]{2,1,0:T(8,128)(2,1)} fusion(bf16[16,128,128]{2,1,0:T(8,128)(2,1)S(1)} %get-tuple-element.186, s32[1024]{0:T(1024)S(1)} %pad_clamp_fusion.10), kind=kCustom, calls=%fused_computation.2.clone.clone.1 | custom fusion | bytes 4194560 | tf_op jit(solution)/shard_map/while/body/jit(_take)/gather | solution.py:43
  52.1 5.2 %multiply_convert_fusion.4 = bf16[64,128,128]{2,1,0:T(8,128)(2,1)} fusion(bf16[64,128,128]{2,1,0:T(8,128)(2,1)} %gather_fusion, bf16[64,128,128]{2,1,0:T(8,128)(2,1)} %gather_fusion.1, pred[64]{0:T(512)(128)(4,1)S(1)} %get-tuple-element.152, pred[64]{0:T(512)(128)(4,1)S(1)} %get-tuple-element.153), kind=kOutput, calls=%fused_computation.5.clone.1 | convolution fusion | flops 272629760 | bytes 6291584 | tf_op jit(solution)/shard_map/while/body/gxb,agb->gxa/dot_general | solution.py:44
  59.5 2.1 %gather_fusion.3 = bf16[64,128,128]{2,1,0:T(8,128)(2,1)} fusion(bf16[16,128,128]{2,1,0:T(8,128)(2,1)S(1)} %get-tuple-element.186, s32[1024]{0:T(1024)S(1)} %pad_clamp_fusion.12), kind=kCustom, calls=%fused_computation.clone.clone.1 | custom fusion | bytes 4194560 | tf_op jit(solution)/shard_map/while/body/jit(_take)/gather | solution.py:43
  62.3 5.1 %fusion.64 = f32[128,128]{1,0:T(8,128)S(1)} fusion(f32[128,128]{1,0:T(8,128)S(1)} %get-tuple-element.171, bf16[64,128,128]{2,1,0:T(8,128)(2,1)} %multiply_convert_fusion.4, bf16[64,128,128]{2,1,0:T(8,128)(2,1)} %gather_fusion.2, bf16[64,128,128]{2,1,0:T(8,128)(2,1)} %gather_fusion.3, pred[64]{0:T(512)(128)(4,1)S(1)} %get-tuple-element.156, ...), kind=kOutput, calls=%fused_computation.20.clone.1 | convolution fusion | flops 542130176 | bytes 6422784 | tf_op jit(solution)/shard_map/while/body/gxa,gay->xy/dot_general | solution.py:56
  68.2 2.1 %gather_fusion = bf16[64,128,128]{2,1,0:T(8,128)(2,1)} fusion(bf16[128,16,128]{2,0,1:T(8,128)(2,1)S(1)} %get-tuple-element.188, s32[1024]{0:T(1024)S(1)} %pad_clamp_fusion.9), kind=kCustom, calls=%fused_computation.3.clone.clone.1 | custom fusion | bytes 4194560 | tf_op jit(solution)/shard_map/while/body/jit(_take)/gather | solution.py:42
  70.4 2.1 %gather_fusion.1 = bf16[64,128,128]{2,1,0:T(8,128)(2,1)} fusion(bf16[16,128,128]{2,1,0:T(8,128)(2,1)S(1)} %get-tuple-element.186, s32[1024]{0:T(1024)S(1)} %pad_clamp_fusion.10), kind=kCustom, calls=%fused_computation.2.clone.clone.1 | custom fusion | bytes 4194560 | tf_op jit(solution)/shard_map/while/body/jit(_take)/gather | solution.py:43
  72.5 5.2 %multiply_convert_fusion.4 = bf16[64,128,128]{2,1,0:T(8,128)(2,1)} fusion(bf16[64,128,128]{2,1,0:T(8,128)(2,1)} %gather_fusion, bf16[64,128,128]{2,1,0:T(8,128)(2,1)} %gather_fusion.1, pred[64]{0:T(512)(128)(4,1)S(1)} %get-tuple-element.152, pred[64]{0:T(512)(128)(4,1)S(1)} %get-tuple-element.153), kind=kOutput, calls=%fused_computation.5.clone.1 | convolution fusion | flops 272629760 | bytes 6291584 | tf_op jit(solution)/shard_map/while/body/gxb,agb->gxa/dot_general | solution.py:44
  79.8 2.1 %gather_fusion.3 = bf16[64,128,128]{2,1,0:T(8,128)(2,1)} fusion(bf16[16,128,128]{2,1,0:T(8,128)(2,1)S(1)} %get-tuple-element.186, s32[1024]{0:T(1024)S(1)} %pad_clamp_fusion.12), kind=kCustom, calls=%fused_computation.clone.clone.1 | custom fusion | bytes 4194560 | tf_op jit(solution)/shard_map/while/body/jit(_take)/gather | solution.py:43
  82.6 5.1 %fusion.64 = f32[128,128]{1,0:T(8,128)S(1)} fusion(f32[128,128]{1,0:T(8,128)S(1)} %get-tuple-element.171, bf16[64,128,128]{2,1,0:T(8,128)(2,1)} %multiply_convert_fusion.4, bf16[64,128,128]{2,1,0:T(8,128)(2,1)} %gather_fusion.2, bf16[64,128,128]{2,1,0:T(8,128)(2,1)} %gather_fusion.3, pred[64]{0:T(512)(128)(4,1)S(1)} %get-tuple-element.156, ...), kind=kOutput, calls=%fused_computation.20.clone.1 | convolution fusion | flops 542130176 | bytes 6422784 | tf_op jit(solution)/shard_map/while/body/gxa,gay->xy/dot_general | solution.py:56
  88.6 2.1 %gather_fusion = bf16[64,128,128]{2,1,0:T(8,128)(2,1)} fusion(bf16[128,16,128]{2,0,1:T(8,128)(2,1)S(1)} %get-tuple-element.188, s32[1024]{0:T(1024)S(1)} %pad_clamp_fusion.9), kind=kCustom, calls=%fused_computation.3.clone.clone.1 | custom fusion | bytes 4194560 | tf_op jit(solution)/shard_map/while/body/jit(_take)/gather | solution.py:42
  90.7 2.1 %gather_fusion.1 = bf16[64,128,128]{2,1,0:T(8,128)(2,1)} fusion(bf16[16,128,128]{2,1,0:T(8,128)(2,1)S(1)} %get-tuple-element.186, s32[1024]{0:T(1024)S(1)} %pad_clamp_fusion.10), kind=kCustom, calls=%fused_computation.2.clone.clone.1 | custom fusion | bytes 4194560 | tf_op jit(solution)/shard_map/while/body/jit(_take)/gather | solution.py:43
  92.8 5.2 %multiply_convert_fusion.4 = bf16[64,128,128]{2,1,0:T(8,128)(2,1)} fusion(bf16[64,128,128]{2,1,0:T(8,128)(2,1)} %gather_fusion, bf16[64,128,128]{2,1,0:T(8,128)(2,1)} %gather_fusion.1, pred[64]{0:T(512)(128)(4,1)S(1)} %get-tuple-element.152, pred[64]{0:T(512)(128)(4,1)S(1)} %get-tuple-element.153), kind=kOutput, calls=%fused_computation.5.clone.1 | convolution fusion | flops 272629760 | bytes 6291584 | tf_op jit(solution)/shard_map/while/body/gxb,agb->gxa/dot_general | solution.py:44
  100.2 2.1 %gather_fusion.3 = bf16[64,128,128]{2,1,0:T(8,128)(2,1)} fusion(bf16[16,128,128]{2,1,0:T(8,128)(2,1)S(1)} %get-tuple-element.186, s32[1024]{0:T(1024)S(1)} %pad_clamp_fusion.12), kind=kCustom, calls=%fused_computation.clone.clone.1 | custom fusion | bytes 4194560 | tf_op jit(solution)/shard_map/while/body/jit(_take)/gather | solution.py:43
  103.0 5.1 %fusion.64 = f32[128,128]{1,0:T(8,128)S(1)} fusion(f32[128,128]{1,0:T(8,128)S(1)} %get-tuple-element.171, bf16[64,128,128]{2,1,0:T(8,128)(2,1)} %multiply_convert_fusion.4, bf16[64,128,128]{2,1,0:T(8,128)(2,1)} %gather_fusion.2, bf16[64,128,128]{2,1,0:T(8,128)(2,1)} %gather_fusion.3, pred[64]{0:T(512)(128)(4,1)S(1)} %get-tuple-element.156, ...), kind=kOutput, calls=%fused_computation.20.clone.1 | convolution fusion | flops 542130176 | bytes 6422784 | tf_op jit(solution)/shard_map/while/body/gxa,gay->xy/dot_general | solution.py:56
  108.7 100.6 %all-gather = bf16[2048,128]{1,0:T(8,128)(2,1)S(1)} all-gather(bf16[128,128]{1,0:T(8,128)(2,1)S(1)} %multiply_convert_fusion.2), channel_id=2, replica_groups=mesh['grp'=2,'had'=16] {'had'}, dimensions={0}, use_global_device_ids=true | all-gather | bytes 557056 | tf_op jit(solution)/shard_map/all_gather | solution.py:65
  (55 shorter events, 21.0 us)
Async XLA Ops:
  0.6 1.4 copy-start
  2.1 11.0 %copy-start.2 = (s32[8,2]{0,1:T(2,128)S(1)}, s32[8,2]{0,1:T(2,128)}, u32[]{:S(2)}) copy-start(s32[8,2]{0,1:T(2,128)} %param.21) | copy-start | bytes 196
  2.1 24.6 %copy-start.1 = (bf16[16,128,128]{2,1,0:T(8,128)(2,1)S(1)}, bf16[16,128,128]{2,1,0:T(8,128)(2,1)}, u32[]{:S(2)}) copy-start(bf16[16,128,128]{2,1,0:T(8,128)(2,1)} %param.15) | copy-start | bytes 1572868
  5.0 21.7 %all-to-all-start = ((bf16[128,16,128]{2,0,1:T(8,128)(2,1)}), bf16[128,16,128]{2,0,1:T(8,128)(2,1)S(1)}, u32[]{:S(2)}, u32[]{:S(2)}) async-start(bf16[128,16,128]{2,0,1:T(8,128)(2,1)} %select_bitcast_fusion), calls=%async_computation | async-start | bytes 1048576 | tf_op jit(solution)/shard_map/all_to_all | solution.py:34
where the time goes:
time: 211 us
  blocking collectives  101 us (48%)
  matrix products  44.2 us (21%)
  local copies, waits for them, and re-layouts  37.9 us (18%)
  waiting for transfers between devices  13.6 us (6%)
  starting transfers between devices  7.41 us (4%)
  other arithmetic  5.68 us (3%)
    all_gather x1, blocking collectives, shards(): shard_rows = lax.all_gather(edge_local, 'had', axis=0, tiled=True)  101 us
    dot_general x4, matrix products, factor(): jnp.einsum('gxb,agb->gxa', resident, gathered, preferred_element_type=jnp...  20.8 us
    dot_general x4, matrix products, accumulate(): jnp.einsum('gxa,gay->xy', left_side, right_side, preferred_element_type=j...  20.3 us
    gather x8, local copies, waits for them, and re-layouts, factor(): resident = jnp.take(sink_slabs, sinks, axis=0)  17.1 us
    gather x8, local copies, waits for them, and re-layouts, factor(): gathered = jnp.take(received, slots, axis=1)  17.1 us
    all_to_all x1, waiting for transfers between devices, shards(): lax.all_to_all(outgoing, 'had', split_axis=1, concat_axis=1, tiled=True)  13.6 us
    all_to_all x1, starting transfers between devices, shards(): lax.all_to_all(outgoing, 'had', split_axis=1, concat_axis=1, tiled=True)  7.41 us
  transfers between devices with their start and end apart: 1, of which 1 were waited for; matrix products, arithmetic and copies ran while one was open for 0% of the time, Pallas kernels for 0%

commit v1 on v0

--- a/solution.py
+++ b/solution.py
@@ -1,12 +1,15 @@
+import functools
 import math
 
 import jax
 import jax.numpy as jnp
 from jax import lax
+from jax.experimental import pallas as pl
+from jax.experimental.pallas import tpu as pltpu
 from jax.sharding import PartitionSpec as P
 
 
-def shards(
+def looped_shards(
     source_slabs,
     sink_slabs,
     perambulators,
@@ -81,9 +84,242 @@
     return (edge_local, pair_products)
 
 
+NT = (((1,), (1,)), ((), ()))
+UNROLL = 8
+
+
+def flip(index, step):
+    flipped = index
+    bit = 1
+    while bit <= step:
+        if step & bit:
+            flipped = flipped + bit * (1 - 2 * (index // bit % 2))
+        bit *= 2
+    return flipped
+
+
+def fused_kernel(
+    n,
+    graphs,
+    pick_ref,
+    slot_ref,
+    graph_sink_ref,
+    count_ref,
+    pair_ref,
+    peram_ref,
+    source_ref,
+    sink_ref,
+    edge_ref,
+    product_ref,
+    outgoing,
+    received,
+    table,
+    edges,
+    graph_ref,
+    send_sem,
+    recv_sem,
+    edge_send_sem,
+    edge_recv_sem,
+):
+    me = lax.axis_index("had")
+    per_device, evecs, _ = source_ref.shape
+    root_scale = 1.0 / math.sqrt(evecs)
+    edge_scale = 1.0 / math.sqrt(evecs * graphs)
+    sinks = sink_ref.shape[0]
+
+    def at(peer):
+        return dict(device_id={"had": peer}, device_id_type=pl.DeviceIdType.MESH)
+
+    barrier = pltpu.get_barrier_semaphore()
+    for step in range(1, n):
+        pl.semaphore_signal(barrier, inc=1, **at(flip(me, step)))
+
+    timeslice = me * per_device // evecs
+    first = peram_ref[timeslice, 0]
+    second = peram_ref[timeslice, 1]
+
+    def rotate(reader):
+        slab = source_ref[pick_ref[0, reader]]
+        half = jnp.dot(first, slab, preferred_element_type=jnp.float32).astype(jnp.bfloat16)
+        turned = lax.dot_general(half, second, NT, preferred_element_type=jnp.float32)
+        return turned.astype(jnp.bfloat16)
+
+    def rotate_step(reader, carry):
+        outgoing[reader] = rotate(reader)
+        return carry
+
+    lax.fori_loop(0, n, rotate_step, 0, unroll=4)
+    received[me] = outgoing[me]
+    pl.semaphore_wait(barrier, n - 1)
+
+    order = list(range(n - 1, 0, -1))
+    copies = []
+    for step in order:
+        peer = flip(me, step)
+        copy = pltpu.make_async_remote_copy(
+            src_ref=outgoing.at[peer],
+            dst_ref=received.at[me],
+            send_sem=send_sem.at[step],
+            recv_sem=recv_sem.at[step],
+            **at(peer),
+        )
+        copy.start()
+        copies.append(copy)
+
+    def index_step(graph, carry):
+        for side in range(2):
+            index = slot_ref[side, graph] * sinks + graph_sink_ref[side, graph]
+            graph_ref[2 * graph + side] = jnp.where(graph < count_ref[0], index, n * sinks)
+        return carry
+
+    lax.fori_loop(0, graphs, index_step, 0, unroll=4)
+    table[n * sinks] = jnp.zeros((evecs, evecs), jnp.bfloat16)
+    rows = 4
+
+    for chip in range(n // 2):
+        for core in range(2):
+            step = 2 * chip + core
+            if step:
+                copies[order.index(step)].wait_recv()
+        base = (flip(me, 2 * chip)) // 2 * 2
+        both = received[pl.ds(base, 2)].reshape(2 * evecs, evecs)
+        for block in range(sinks // rows):
+            left = sink_ref[block * rows : (block + 1) * rows].reshape(rows * evecs, evecs)
+            product = lax.dot_general(left, both, NT, preferred_element_type=jnp.float32)
+            scaled = (product * root_scale).astype(jnp.bfloat16)
+            for core in range(2):
+                part = scaled[:, core * evecs : (core + 1) * evecs].reshape(rows, evecs, evecs)
+                table[pl.ds((base + core) * sinks + block * rows, rows)] = part
+    for copy in copies:
+        copy.wait_send()
+
+    def graph_step(block, total):
+        for inner in range(0, UNROLL, 2):
+            index = 2 * (block * UNROLL + inner)
+            left = jnp.concatenate([table[graph_ref[index]], table[graph_ref[index + 2]]], axis=1)
+            right = jnp.concatenate(
+                [table[graph_ref[index + 1]], table[graph_ref[index + 3]]], axis=0
+            )
+            total = total + jnp.dot(left, right, preferred_element_type=jnp.float32)
+        return total
+
+    total = lax.fori_loop(
+        0, graphs // UNROLL, graph_step, jnp.zeros((evecs, evecs), jnp.float32)
+    )
+    edge = (total * edge_scale).astype(jnp.bfloat16)
+    edge_ref[0] = edge
+    edges[me] = edge
+
+    sent = []
+
+    def pass_on(step, peer_step, kind):
+        owner = flip(me, step)
+        slot = step if kind else peer_step
+        copy = pltpu.make_async_remote_copy(
+            src_ref=edges.at[owner],
+            dst_ref=edges.at[owner],
+            send_sem=edge_send_sem.at[kind, slot],
+            recv_sem=edge_recv_sem.at[step ^ peer_step],
+            **at(flip(me, peer_step)),
+        )
+        copy.start()
+        sent.append(copy)
+
+    def arrived(step):
+        pltpu.make_async_remote_copy(
+            src_ref=edges.at[me],
+            dst_ref=edges.at[flip(me, step)],
+            send_sem=edge_send_sem.at[0, 0],
+            recv_sem=edge_recv_sem.at[step],
+            **at(flip(me, 1)),
+        ).wait_recv()
+
+    for step in range(n - 4, 0, -4):
+        pass_on(0, step, 0)
+    pass_on(0, 2, 1)
+    pass_on(0, 1, 2)
+    for step in range(4, n, 4):
+        arrived(step)
+        pass_on(step, 2, 1)
+        pass_on(step, 1, 2)
+    for step in range(2, n, 4):
+        arrived(step)
+        pass_on(step, 1, 2)
+    for step in range(1, n, 2):
+        arrived(step)
+    for copy in sent:
+        copy.wait_send()
+
+    for pair in range(product_ref.shape[0]):
+        product = jnp.dot(
+            edges[pair_ref[0, pair]],
+            edges[pair_ref[1, pair]],
+            preferred_element_type=jnp.float32,
+        )
+        product_ref[pair] = (product * root_scale).astype(jnp.bfloat16)
+
+
+def fused_shards(
+    n,
+    source_slabs,
+    sink_slabs,
+    perambulators,
+    send_pick,
+    graph_slot,
+    graph_sink,
+    graph_count,
+    pair_list,
+):
+    sinks, evecs, _ = sink_slabs.shape
+    graphs = graph_slot.shape[1]
+    vmem = pl.BlockSpec(memory_space=pltpu.VMEM)
+    smem = pl.BlockSpec(memory_space=pltpu.SMEM)
+    slab = (evecs, evecs)
+    return pl.pallas_call(
+        functools.partial(fused_kernel, n, graphs),
+        out_shape=(
+            jax.ShapeDtypeStruct((1, *slab), jnp.bfloat16),
+            jax.ShapeDtypeStruct((pair_list.shape[0], *slab), jnp.bfloat16),
+        ),
+        in_specs=[smem, smem, smem, smem, smem, vmem, vmem, vmem],
+        out_specs=(vmem, vmem),
+        scratch_shapes=[
+            pltpu.VMEM((n, *slab), jnp.bfloat16),
+            pltpu.VMEM((n, *slab), jnp.bfloat16),
+            pltpu.VMEM((n * sinks + 1, *slab), jnp.bfloat16),
+            pltpu.VMEM((n, *slab), jnp.bfloat16),
+            pltpu.SMEM((2 * graphs,), jnp.int32),
+            pltpu.SemaphoreType.DMA((n,)),
+            pltpu.SemaphoreType.DMA((n,)),
+            pltpu.SemaphoreType.DMA((3, n)),
+            pltpu.SemaphoreType.DMA((n,)),
+        ],
+        compiler_params=pltpu.CompilerParams(collective_id=0, has_side_effects=True),
+        name="contraction",
+    )(
+        send_pick,
+        graph_slot[0].T,
+        graph_sink[0].T,
+        graph_count,
+        pair_list.T,
+        perambulators,
+        source_slabs,
+        sink_slabs,
+    )
+
+
+def shards(readers, source_slabs, sink_slabs, perambulators, *tables):
+    slabs = sink_slabs.shape[0]
+    graphs = tables[1].shape[1]
+    power = readers & (readers - 1) == 0 and readers % 4 == 0
+    if power and readers * slabs <= 2 * graphs and graphs % UNROLL == 0 and slabs % 4 == 0:
+        return fused_shards(readers, source_slabs, sink_slabs, perambulators, *tables)
+    return looped_shards(source_slabs, sink_slabs, perambulators, *tables)
+
+
 def solution(mesh):
     return jax.shard_map(
-        shards,
+        functools.partial(shards, mesh.shape["had"]),
         mesh=mesh,
         in_specs=(
             P(("grp", "had"), None, None),

time: 211 us -> 50 us (0.24)
  blocking collectives: 101 us -> 0 us
  Pallas kernels: 0 us -> 45.5 us
  matrix products: 44.2 us -> 0 us
  local copies, waits for them, and re-layouts: 37.9 us -> 3.05 us
  waiting for transfers between devices: 13.6 us -> 0 us
  starting transfers between devices: 7.41 us -> 0 us
  other arithmetic: 5.68 us -> 0 us
    all_gather x1 -> x0, blocking collectives: 101 us -> none  [shards(): shard_rows = lax.all_gather(edge_local, 'had', axis=0, tiled=True)]
    pallas_call x0 -> x1, Pallas kernels: none -> 45.5 us  [fused_shards(): pl.pallas_call(functools.partial(fused_kernel, n, graphs), out_shape=(jax...]
    dot_general x12 -> x0, matrix products: 44.2 us -> none  [the longest x4 20.8 us: factor(): jnp.einsum('gxb,agb->gxa', resident, gathered, preferred_element_type=jnp...]
    gather x17 -> x0, local copies, waits for them, and re-layouts: 34.8 us -> none  [the longest x8 17.1 us: factor(): resident = jnp.take(sink_slabs, sinks, axis=0)]
    all_to_all x1 -> x0, waiting for transfers between devices: 13.6 us -> none  [shards(): lax.all_to_all(outgoing, 'had', split_axis=1, concat_axis=1, tiled=True)]
    all_to_all x1 -> x0, starting transfers between devices: 7.41 us -> none  [shards(): lax.all_to_all(outgoing, 'had', split_axis=1, concat_axis=1, tiled=True)]
    dynamic_slice x4 -> x0, local copies, waits for them, and re-layouts: 3.09 us -> none  [accumulate(): slots = lax.dynamic_slice_in_dim(slot_table, offset, block_width, 0)]
    unnamed x6 -> x2, local copies, waits for them, and re-layouts: 0.02 us -> 3.05 us
  transfers between devices with their start and end apart: 1 -> 0, of which waited for: 1 -> 0; matrix products, arithmetic and copies ran while one was open for 0% -> 0% of each run, Pallas kernels for 0% -> 0%
where the time goes in v1:
time: 50 us; the launch traced here: 49.8 us
  Pallas kernels  45.5 us (91%)
  local copies, waits for them, and re-layouts  3.05 us (6%)
  between operations  1.29 us (3%)
    pallas_call x1, Pallas kernels, fused_shards(): pl.pallas_call(functools.partial(fused_kernel, n, graphs), out_shape=(jax...  45.5 us
    unnamed x2, local copies, waits for them, and re-layouts  3.05 us

profile of v1, /device:TPU:0, one launch (start us, length us, event | category | flops | bytes accessed | tf_op | source)
XLA Modules:
  0.0 49.8 jit_solution(14746714059417451494)
XLA Ops:
  1.3 45.5 %contraction.1 = (bf16[1,128,128]{2,1,0:T(8,128)(2,1)}, bf16[8,128,128]{2,1,0:T(8,128)(2,1)}) custom-call(s32[1,16]{1,0:T(1,128)} %pick_ref.1, s32[2,512]{1,0:T(2,128)} %bitcast.7, s32[2,512]{1,0:T(2,128)} %bitcast.8, s32[1]{0:T(128)S(6)} %copy.12.count_ref, s32[2,8]{1,0:T(2,128)} %bitcast.9, bf16[2,2,128,128]{3,2,1,0:T(8,128)(2,1)} %peram_ref.1, ...), custom_call_target="tpu_custom_call" | custom-call | tf_op jit(solution)/shard_map/contraction/pallas_call | solution.py:278
  46.7 1.4 %copy.13 = bf16[1,128,128]{2,1,0:T(8,128)(2,1)} copy(bf16[1,128,128]{2,1,0:T(8,128)(2,1)} %get-tuple-element.4) | data formatting | bytes 65536
  48.1 1.7 %copy.14 = bf16[8,128,128]{2,1,0:T(8,128)(2,1)} copy(bf16[8,128,128]{2,1,0:T(8,128)(2,1)} %get-tuple-element.5) | data formatting | bytes 524288

commit v2 on v1

--- a/solution.py
+++ b/solution.py
@@ -85,7 +85,7 @@
 
 
 NT = (((1,), (1,)), ((), ()))
-UNROLL = 8
+UNROLL = 128
 
 
 def flip(index, step):
@@ -105,17 +105,18 @@
     slot_ref,
     graph_sink_ref,
     count_ref,
-    pair_ref,
+    peram_in,
+    source_in,
+    sink_in,
+    edges,
+    outgoing,
+    received,
+    table,
+    graph_ref,
     peram_ref,
     source_ref,
     sink_ref,
-    edge_ref,
-    product_ref,
-    outgoing,
-    received,
-    table,
-    edges,
-    graph_ref,
+    load_sem,
     send_sem,
     recv_sem,
     edge_send_sem,
@@ -134,6 +135,15 @@
     for step in range(1, n):
         pl.semaphore_signal(barrier, inc=1, **at(flip(me, step)))
 
+    peram_load = pltpu.make_async_copy(peram_in, peram_ref, load_sem.at[0])
+    source_load = pltpu.make_async_copy(source_in, source_ref, load_sem.at[1])
+    sink_load = pltpu.make_async_copy(sink_in, sink_ref, load_sem.at[2])
+    peram_load.start()
+    source_load.start()
+    sink_load.start()
+    peram_load.wait()
+    source_load.wait()
+
     timeslice = me * per_device // evecs
     first = peram_ref[timeslice, 0]
     second = peram_ref[timeslice, 1]
@@ -152,7 +162,7 @@
     received[me] = outgoing[me]
     pl.semaphore_wait(barrier, n - 1)
 
-    order = list(range(n - 1, 0, -1))
+    order = list(range(1, n))
     copies = []
     for step in order:
         peer = flip(me, step)
@@ -175,6 +185,7 @@
     lax.fori_loop(0, graphs, index_step, 0, unroll=4)
     table[n * sinks] = jnp.zeros((evecs, evecs), jnp.bfloat16)
     rows = 4
+    sink_load.wait()
 
     for chip in range(n // 2):
         for core in range(2):
@@ -194,20 +205,19 @@
         copy.wait_send()
 
     def graph_step(block, total):
-        for inner in range(0, UNROLL, 2):
-            index = 2 * (block * UNROLL + inner)
-            left = jnp.concatenate([table[graph_ref[index]], table[graph_ref[index + 2]]], axis=1)
-            right = jnp.concatenate(
-                [table[graph_ref[index + 1]], table[graph_ref[index + 3]]], axis=0
-            )
-            total = total + jnp.dot(left, right, preferred_element_type=jnp.float32)
-        return total
+        first = 2 * UNROLL * block
+        left = [table[graph_ref[first + 2 * graph]] for graph in range(UNROLL)]
+        right = [table[graph_ref[first + 2 * graph + 1]] for graph in range(UNROLL)]
+        return total + jnp.dot(
+            jnp.concatenate(left, axis=1),
+            jnp.concatenate(right, axis=0),
+            preferred_element_type=jnp.float32,
+        )
 
     total = lax.fori_loop(
         0, graphs // UNROLL, graph_step, jnp.zeros((evecs, evecs), jnp.float32)
     )
     edge = (total * edge_scale).astype(jnp.bfloat16)
-    edge_ref[0] = edge
     edges[me] = edge
 
     sent = []
@@ -250,6 +260,11 @@
     for copy in sent:
         copy.wait_send()
 
+
+def pair_kernel(pair_ref, edges, edge_ref, product_ref):
+    me = lax.axis_index("had")
+    root_scale = 1.0 / math.sqrt(edges.shape[1])
+    edge_ref[0] = edges[me]
     for pair in range(product_ref.shape[0]):
         product = jnp.dot(
             edges[pair_ref[0, pair]],
@@ -273,22 +288,23 @@
     sinks, evecs, _ = sink_slabs.shape
     graphs = graph_slot.shape[1]
     vmem = pl.BlockSpec(memory_space=pltpu.VMEM)
+    hbm = pl.BlockSpec(memory_space=pl.ANY)
     smem = pl.BlockSpec(memory_space=pltpu.SMEM)
     slab = (evecs, evecs)
-    return pl.pallas_call(
+    edges = pl.pallas_call(
         functools.partial(fused_kernel, n, graphs),
-        out_shape=(
-            jax.ShapeDtypeStruct((1, *slab), jnp.bfloat16),
-            jax.ShapeDtypeStruct((pair_list.shape[0], *slab), jnp.bfloat16),
-        ),
-        in_specs=[smem, smem, smem, smem, smem, vmem, vmem, vmem],
-        out_specs=(vmem, vmem),
+        out_shape=jax.ShapeDtypeStruct((n, *slab), jnp.bfloat16),
+        in_specs=[smem, smem, smem, smem, hbm, hbm, hbm],
+        out_specs=vmem,
         scratch_shapes=[
             pltpu.VMEM((n, *slab), jnp.bfloat16),
             pltpu.VMEM((n, *slab), jnp.bfloat16),
             pltpu.VMEM((n * sinks + 1, *slab), jnp.bfloat16),
-            pltpu.VMEM((n, *slab), jnp.bfloat16),
             pltpu.SMEM((2 * graphs,), jnp.int32),
+            pltpu.VMEM(perambulators.shape, jnp.bfloat16),
+            pltpu.VMEM(source_slabs.shape, jnp.bfloat16),
+            pltpu.VMEM(sink_slabs.shape, jnp.bfloat16),
+            pltpu.SemaphoreType.DMA((3,)),
             pltpu.SemaphoreType.DMA((n,)),
             pltpu.SemaphoreType.DMA((n,)),
             pltpu.SemaphoreType.DMA((3, n)),
@@ -301,11 +317,20 @@
         graph_slot[0].T,
         graph_sink[0].T,
         graph_count,
-        pair_list.T,
         perambulators,
         source_slabs,
         sink_slabs,
     )
+    return pl.pallas_call(
+        pair_kernel,
+        out_shape=(
+            jax.ShapeDtypeStruct((1, *slab), jnp.bfloat16),
+            jax.ShapeDtypeStruct((pair_list.shape[0], *slab), jnp.bfloat16),
+        ),
+        in_specs=[smem, vmem],
+        out_specs=(vmem, vmem),
+        name="pairs",
+    )(pair_list.T, edges)
 
 
 def shards(readers, source_slabs, sink_slabs, perambulators, *tables):

time: 50 us -> 39 us (0.78)
  Pallas kernels: 45.5 us -> 37.5 us
  local copies, waits for them, and re-layouts: 3.05 us -> 0 us
    pallas_call x1 -> x2, Pallas kernels: 45.5 us -> 37.5 us  [the longest x1 35.5 us: fused_shards(): pl.pallas_call(functools.partial(fused_kernel, n, graphs), out_shape=jax....]
    unnamed x2 -> x0, local copies, waits for them, and re-layouts: 3.05 us -> none
where the time goes in v2:
time: 39 us; the launch traced here: 38.8 us
  Pallas kernels  37.5 us (96%)
  between operations  1.29 us (3%)
    pallas_call x1, Pallas kernels, fused_shards(): pl.pallas_call(functools.partial(fused_kernel, n, graphs), out_shape=jax....  35.5 us
    pallas_call x1, Pallas kernels, fused_shards(): pl.pallas_call(pair_kernel, out_shape=(jax.ShapeDtypeStruct((1, *slab), j...  1.98 us

profile of v2, /device:TPU:0, one launch (start us, length us, event | category | flops | bytes accessed | tf_op | source)
XLA Modules:
  0.0 38.8 jit_solution(2201225257190539487)
XLA Ops:
  1.3 35.5 %contraction.1.edges = bf16[16,128,128]{2,1,0:T(8,128)(2,1)} custom-call(s32[1,16]{1,0:T(1,128)} %pick_ref.1, s32[2,512]{1,0:T(2,128)} %bitcast.7, s32[2,512]{1,0:T(2,128)} %bitcast.8, s32[1]{0:T(128)S(6)} %copy.10.count_ref, bf16[2,2,128,128]{3,2,1,0:T(8,128)(2,1)} %peram_in.1, bf16[16,128,128]{2,1,0:T(8,128)(2,1)} %source_in.1, bf16[16,128,128]{2,1,0:T(8,128)(2,1)} %sink_in.1), custom_call_target="tpu_custom_call" | custom-call | tf_op jit(solution)/shard_map/contraction/pallas_call | solution.py:294
  36.8 2.0 %pairs.1 = (bf16[1,128,128]{2,1,0:T(8,128)(2,1)}, bf16[8,128,128]{2,1,0:T(8,128)(2,1)}) custom-call(s32[2,8]{1,0:T(2,128)} %bitcast.9, bf16[16,128,128]{2,1,0:T(8,128)(2,1)} %contraction.1.edges), custom_call_target="tpu_custom_call" | custom-call | tf_op jit(solution)/shard_map/pairs/pallas_call | solution.py:324

commit v3 on v2

--- a/solution.py
+++ b/solution.py
@@ -85,7 +85,7 @@
 
 
 NT = (((1,), (1,)), ((), ()))
-UNROLL = 128
+UNROLL = 256
 
 
 def flip(index, step):
@@ -244,15 +244,10 @@
             **at(flip(me, 1)),
         ).wait_recv()
 
-    for step in range(n - 4, 0, -4):
+    for step in range(n - 2, 0, -2):
         pass_on(0, step, 0)
-    pass_on(0, 2, 1)
     pass_on(0, 1, 2)
-    for step in range(4, n, 4):
-        arrived(step)
-        pass_on(step, 2, 1)
-        pass_on(step, 1, 2)
-    for step in range(2, n, 4):
+    for step in range(2, n, 2):
         arrived(step)
         pass_on(step, 1, 2)
     for step in range(1, n, 2):

time: 39 us -> 38.1 us (0.977)
  Pallas kernels: 37.5 us -> 36.6 us
    pallas_call x1, Pallas kernels: 35.5 us -> 34.6 us  [fused_shards(): pl.pallas_call(functools.partial(fused_kernel, n, graphs), out_shape=jax....]
where the time goes in v3:
time: 38.1 us; the launch traced here: 37.9 us
  Pallas kernels  36.6 us (96%)
  between operations  1.29 us (3%)
    pallas_call x1, Pallas kernels, fused_shards(): pl.pallas_call(functools.partial(fused_kernel, n, graphs), out_shape=jax....  34.6 us
    pallas_call x1, Pallas kernels, fused_shards(): pl.pallas_call(pair_kernel, out_shape=(jax.ShapeDtypeStruct((1, *slab), j...  1.98 us

profile of v3, /device:TPU:0, one launch (start us, length us, event | category | flops | bytes accessed | tf_op | source)
XLA Modules:
  0.0 37.9 jit_solution(9277190825515009588)
XLA Ops:
  1.3 34.6 %contraction.1.edges = bf16[16,128,128]{2,1,0:T(8,128)(2,1)} custom-call(s32[1,16]{1,0:T(1,128)} %pick_ref.1, s32[2,512]{1,0:T(2,128)} %bitcast.7, s32[2,512]{1,0:T(2,128)} %bitcast.8, s32[1]{0:T(128)S(6)} %copy.10.count_ref, bf16[2,2,128,128]{3,2,1,0:T(8,128)(2,1)} %peram_in.1, bf16[16,128,128]{2,1,0:T(8,128)(2,1)} %source_in.1, bf16[16,128,128]{2,1,0:T(8,128)(2,1)} %sink_in.1), custom_call_target="tpu_custom_call" | custom-call | tf_op jit(solution)/shard_map/contraction/pallas_call | solution.py:289
  35.9 2.0 %pairs.1 = (bf16[1,128,128]{2,1,0:T(8,128)(2,1)}, bf16[8,128,128]{2,1,0:T(8,128)(2,1)}) custom-call(s32[2,8]{1,0:T(2,128)} %bitcast.9, bf16[16,128,128]{2,1,0:T(8,128)(2,1)} %contraction.1.edges), custom_call_target="tpu_custom_call" | custom-call | tf_op jit(solution)/shard_map/pairs/pallas_call | solution.py:319
